TPU v7x, 128 devices: a whole 4x4x4 slice. The times are simulated.
128 devices in a mesh: angle: 16 (over y, x), block: 8 (over z, core).
Axes of the slice: x: 4, y: 4, z: 4, core: 2. Of those that a mesh axis runs over, the one named last changes fastest.
Arguments:
- object_field: float32 [32, 2, 512, 512], P(None, None, 'block'), may hold values from -1.5 to 1.5
- shears: int32 [16, 32], P('angle'), may hold values from -16 to 16, as said below
- positions: int32 [16, 8, 2], P('angle', 'block'), may hold values from 0 to 511
- measured: bfloat16 [16, 8, 512, 512], P('angle', 'block'), may hold values from 0 to 2
- probe_field: float32 [2, 512, 512], replicated
- kappa_field: float32 [16, 512, 512], P('angle'), may hold values from 0.01 to 0.1
Outputs:
- updated_object: float32 [32, 2, 512, 512], P(None, None, 'block')
Inputs may be any that keep to these rules, and one draw needn't show every extreme that they name: `shears`: each angle's row offset of each slice; the values -16 and 16 occur in every draw.
All inputs are finite; a program needn't handle non-finite values.
Results may differ from a plain program's by a relative error of at most 0.0003.
Values sent between devices are 32-bit elements; how exact they have to be, the bound alone decides.
No kernel may reach another device: no remote copies, remote signals or barrier semaphores. Data moves between devices by JAX's collectives and lax.ppermute only.
A program may use at most 192 MiB of HBM per device.

v0:
```python
import jax
import jax.numpy as jnp
from jax import lax
from jax.sharding import PartitionSpec as P

NX = 512
NY = 512
STEPS = 2
SH = 16


def with_halo(x, sides, width):
    for axis, dim in sides:
        count, length = (lax.axis_size(axis), x.shape[dim])
        up = [(i, (i + 1) % count) for i in range(count)]
        down = [(j, i) for i, j in up]
        last = lax.slice_in_dim(x, length - width, length, axis=dim)
        first = lax.slice_in_dim(x, 0, width, axis=dim)
        before = lax.ppermute(last, axis, up)
        after = lax.ppermute(first, axis, down)
        x = jnp.concatenate([before, x, after], axis=dim)
    return x


def laplace(field):
    return (
        jnp.roll(field, 1, -2)
        + jnp.roll(field, -1, -2)
        + jnp.roll(field, 1, -1)
        + jnp.roll(field, -1, -1)
        - 4.0 * field
    )


def frame_loss(projected, probe_field, kappa_row, offset, observed):
    window = jnp.roll(projected, (-offset[0], -offset[1]), axis=(1, 2))
    real_part = probe_field[0] * window[0] - probe_field[1] * window[1]
    imag_part = probe_field[0] * window[1] + probe_field[1] * window[0]
    for step in range(STEPS):
        real_part, imag_part = (
            real_part - kappa_row * laplace(imag_part),
            imag_part + kappa_row * laplace(real_part),
        )
    misfit = real_part * real_part + imag_part * imag_part - observed.astype(jnp.float32)
    return 0.5 * jnp.sum(misfit * misfit)


def per_device(object_field, shears, positions, measured, probe_field, kappa_field):
    strip_rows = object_field.shape[2]
    shear_row = shears[0]
    extended = with_halo(object_field, (("block", 2),), SH)

    def slice_rows(slab, amount):
        return lax.dynamic_slice_in_dim(slab, SH + amount, strip_rows, 1)

    own_strip = jnp.sum(jax.vmap(slice_rows)(extended, shear_row), axis=0)
    projected = lax.all_gather(own_strip, "block", axis=1, tiled=True)
    intensity = probe_field[0] * probe_field[0] + probe_field[1] * probe_field[1]
    kappa_row = kappa_field[0]

    def per_frame(totals, frame_in):
        offset, observed = frame_in
        grads = jax.grad(frame_loss)(projected, probe_field, kappa_row, offset, observed)
        weight = jnp.roll(intensity, (offset[0], offset[1]), axis=(0, 1))
        return (totals + jnp.concatenate([grads, weight[None]], 0), None)

    totals, _ = lax.scan(
        per_frame, jnp.zeros((3, NX, NY), jnp.float32), (positions[0], measured[0])
    )
    strip_totals = lax.psum_scatter(totals, "block", scatter_dimension=1, tiled=True)
    gradient_rim = with_halo(strip_totals, (("block", 1),), SH)

    def unshear_rows(rim_block, amount):
        return lax.dynamic_slice_in_dim(rim_block, SH - amount, strip_rows, 1)

    unsheared = jax.vmap(lambda amount: unshear_rows(gradient_rim, amount))(shear_row)
    summed = lax.psum(unsheared, "angle")
    return object_field - summed[:, :2] / (summed[:, 2:3] + 1.0)


def solution(mesh):
    placed = (
        P(None, None, "block", None),
        P("angle", None),
        P("angle", "block", None),
        P("angle", "block", None, None),
        P(),
        P("angle", None, None),
    )
    return jax.shard_map(
        per_device,
        mesh=mesh,
        in_specs=placed,
        out_specs=P(None, None, "block", None),
        check_vma=False,
    )
```

profile of v0, /device:TPU:1, one launch (start us, length us, event | category | flops | bytes accessed | tf_op | source)
XLA Modules:
  0.0 588.4 jit_solution(2454463777330651448)
XLA Ops:
  6.5 14.3 %copy.27 = f32[32,2,64,512]{3,1,0,2:T(2,128)S(1)} copy(f32[32,2,64,512]{3,2,1,0:T(8,128)} %param.6) | data formatting | bytes 16777216 | tf_op args[0]
  20.9 2.3 fusion.41
  23.2 3.0 collective-permute-start
  26.2 23.0 %collective-permute-done = f32[32,2,16,512]{3,1,0,2:T(2,128)S(1)} collective-permute-done((f32[32,2,16,512]{3,1,0,2:T(2,128)S(1)}, f32[32,2,16,512]{3,1,0,2:T(2,128)S(1)}, u32[]{:S(2)}, u32[]{:S(2)}) %collective-permute-start) | collective-permute-done | bytes 2097184 | tf_op jit(solution)/shard_map/ppermute | solution.py:19
  49.2 2.5 collective-permute-done.1
  51.7 26.0 %pad_maximum_fusion = f32[32,2,96,512]{3,1,0,2:T(2,128)} fusion(f32[32,2,16,512]{3,1,0,2:T(2,128)S(1)} %collective-permute-done.1, f32[32,2,64,512]{3,1,0,2:T(2,128)S(1)} %copy.27, f32[32,2,16,512]{3,1,0,2:T(2,128)S(1)} %collective-permute-done), kind=kLoop, calls=%fused_computation.2 | loop fusion | flops 6291456 | bytes 25165824 | tf_op jit(solution)/shard_map/concatenate | solution.py:21
  77.7 16.2 %gather_fusion.1 = f32[32,2,64,512]{3,1,2,0:T(2,128)} fusion(f32[32,2,96,512]{3,1,0,2:T(2,128)} %pad_maximum_fusion, s32[32]{0:T(128)S(1)} %get-tuple-element.115), kind=kCustom, calls=%fused_computation.1 | custom fusion | bytes 16777728 | tf_op jit(solution)/shard_map/vmap()/gather | solution.py:54
  94.0 6.8 %reduce_sum.9 = f32[2,64,512]{2,0,1:T(2,128)} reduce(f32[32,2,64,512]{3,1,2,0:T(2,128)} %gather_fusion.1, f32[]{:T(128)} %constant.99.clone.1), dimensions={0}, to_apply=%region_0.0 | reduce | flops 2031616 | bytes 8650756 | tf_op jit(solution)/shard_map/reduce_sum | solution.py:56
  101.1 0.6 fusion.75
  106.7 21.5 %all-gather.2.cloned.1.call-done = f32[2,512,512]{2,0,1:T(2,128)} async-done(((f32[2,64,512]{2,0,1:T(2,128)}), f32[2,512,512]{2,0,1:T(2,128)}) %all-gather.2.cloned.1.call-update) | async-done | bytes 2097168 | tf_op jit(solution)/shard_map/all_gather | solution.py:57
  128.2 5.8 fusion.3
  133.9 4.5 fusion.2
  138.4 1.6 fusion.42
  140.0 0.5 fusion.27
  141.3 0.4 copy-done
  141.8 12.8 %fusion.16 = (f32[512,512]{1,0:T(8,128)S(1)}, f32[512,512]{1,0:T(8,128)S(1)}) fusion(f32[511,512]{1,0:T(8,128)S(1)} %get-tuple-element.111, f32[1,512]{1,0:T(1,128)S(1)} %get-tuple-element.113, f32[1,512]{1,0:T(1,128)S(1)} %get-tuple-element.112, f32[511,512]{1,0:T(8,128)S(1)} %get-tuple-element.110, f32[512,511]{1,0:T(8,128)S(1)} %get-tuple-element.107, ...), kind=kLoop, calls=%fused_computation.35 | loop fusion | flops 3670016 | bytes 12582912 | tf_op jit(solution)/shard_map/while/body/eval_jaxpr/jvp()/sub | solution.py:41
  154.8 0.7 fusion.62
  155.9 1.0 fusion.11
  157.9 2.3 bitcast_multiply_fusion.5
  160.3 0.4 bitcast_multiply_fusion.4
  161.4 1.2 bitcast_multiply_fusion.3
  164.1 2.4 fusion.34
  167.5 1.0 fusion.35
  168.5 0.5 fusion.31
  169.0 0.5 pad_add_fusion
  169.5 1.6 copy.31
  171.1 3.1 broadcast_in_dim.37
  174.2 96.8 %dynamic_update_slice.10 = f32[2,512,1024]{2,0,1:T(2,128)} dynamic-update-slice(f32[2,512,1024]{2,0,1:T(2,128)} %broadcast_in_dim.37, f32[2,512,512]{2,0,1:T(2,128)S(1)} %copy.31, s32[]{:T(128)} %constant.100.clone.1, s32[]{:T(128)} %constant.100.clone.1, s32[]{:T(128)S(6)} %select_n.79) | dynamic-update-slice | bytes 4194308 | tf_op jit(solution)/shard_map/while/body/eval_jaxpr/transpose(jvp(jit(_roll_dynamic)))/dynamic_update_slice | solution.py:36
  271.1 1.1 broadcast_in_dim.36
  272.2 1.1 copy-done.2
  273.3 1.2 fusion.4
  274.5 1.1 slice_add_fusion.1
  275.6 0.5 fusion.6
  276.1 0.6 fusion.5
  276.7 0.7 broadcast_in_dim.42
  277.4 3.9 pad_maximum_fusion.1
  281.4 0.6 dynamic-slice
  282.6 70.1 %all-reduce.42.cloned.1.call-done = f32[3,512,512]{2,0,1:T(4,128)} async-done(((f32[3,512,512]{2,0,1:T(4,128)}), f32[3,512,512]{2,0,1:T(4,128)}) %all-reduce.42.cloned.1.call-update) | async-done | bytes 3145744
  352.6 1.0 constant_dynamic-slice_fusion.1
  353.7 0.9 collective-permute-start.2
  354.5 1.6 collective-permute-start.3
  356.1 1.1 constant_dynamic-slice_fusion.2
  357.3 1.7 collective-permute-done.3
  359.1 12.3 %gather_fusion = f32[32,3,64,512]{3,1,2,0:T(4,128)} fusion(f32[3,96,512]{2,0,1:T(4,128)S(1)} %pad_maximum_fusion.2, s32[32]{0:T(128)S(1)} %get-tuple-element.114), kind=kCustom, calls=%fused_computation | custom fusion | bytes 25166208 | tf_op jit(solution)/shard_map/vmap()/gather | solution.py:74
  371.4 15.5 %copy.32 = f32[32,3,64,512]{3,2,1,0:T(8,128)} copy(f32[32,3,64,512]{3,1,2,0:T(4,128)} %gather_fusion) | data formatting | bytes 25165824 | tf_op jit(solution)/shard_map/vmap()/gather | solution.py:74
  387.0 182.0 %all-reduce.40.cloned.1.call-done = f32[32,3,64,512]{3,2,1,0:T(8,128)} async-done(((f32[32,3,64,512]{3,2,1,0:T(8,128)}), f32[32,3,64,512]{3,2,1,0:T(8,128)}) %all-reduce.40.cloned.1.call-update) | async-done | bytes 12582928 | tf_op jit(solution)/shard_map/psum | solution.py:77
  569.0 2.9 fusion.1
  571.9 9.6 %fusion = f32[32,2,64,512]{3,2,1,0:T(8,128)} fusion(f32[32,2,64,512]{3,2,1,0:T(8,128)} %param.6, f32[32,3,64,512]{3,2,1,0:T(8,128)} %all-reduce.40.cloned.1.call-done, f32[32,64,512]{2,1,0:T(8,128)S(1)} %fusion.1), kind=kLoop, calls=%fused_computation.4 | loop fusion | flops 4194304 | bytes 29360128 | tf_op jit(solution)/shard_map/sub | solution.py:78
  (50 shorter events, 6.1 us)
Async XLA Ops:
  6.5 121.6 %all-gather.2.cloned.1.call-start = ((), (), s32[]{:S(2)}) async-start(), calls=%async_computation | async-start | bytes 2359296 | tf_op jit(solution)/shard_map/all_gather | solution.py:57
  20.9 5.4 copy-start.5
  23.2 26.0 %collective-permute-start = (f32[32,2,16,512]{3,1,0,2:T(2,128)S(1)}, f32[32,2,16,512]{3,1,0,2:T(2,128)S(1)}, u32[]{:S(2)}, u32[]{:S(2)}) collective-permute-start(f32[32,2,16,512]{3,1,0,2:T(2,128)S(1)} %get-tuple-element.41), channel_id=1, source_target_pairs={{0,1},{1,2},{2,3},{3,4},{4,5},{5,6},{6,7},{7,0},{8,9},{9,10},{10,1... | collective-permute-start | bytes 6291464 | tf_op jit(solution)/shard_map/ppermute | solution.py:19
  26.2 25.5 %collective-permute-start.1 = (f32[32,2,16,512]{3,1,0,2:T(2,128)S(1)}, f32[32,2,16,512]{3,1,0,2:T(2,128)S(1)}, u32[]{:S(2)}, u32[]{:S(2)}) collective-permute-start(f32[32,2,16,512]{3,1,0,2:T(2,128)S(1)} %get-tuple-element.42), channel_id=1, source_target_pairs={{1,0},{2,1},{3,2},{4,3},{5,4},{6,5},{7,6},{0,7},{9,8},{10,9},{11,1... | collective-permute-start | bytes 6291464 | tf_op jit(solution)/shard_map/ppermute | solution.py:20
  94.0 7.2 %copy-start.4 = (s32[1,1,2]{2,1,0:T(1,128)S(1)}, s32[1,1,2]{2,1,0:T(1,128)}, u32[]{:S(2)}) copy-start(s32[1,1,2]{2,1,0:T(1,128)} %param.8) | copy-start | bytes 28
  100.8 251.8 %all-reduce.42.cloned.1.call-start = ((), (), s32[]{:S(2)}) async-start(), calls=%async_computation.2 | async-start | bytes 8388608
  133.9 6.1 %copy-start.1 = (f32[2,512,512]{2,1,0:T(8,128)S(1)}, f32[2,512,512]{2,1,0:T(8,128)}, u32[]{:S(2)}) copy-start(f32[2,512,512]{2,1,0:T(8,128)} %param.10) | copy-start | bytes 6291460
  140.5 1.2 copy-start
  156.9 1.0 copy-start.3
  271.1 2.2 copy-start.2
  277.4 4.0 copy-start.6
  281.4 287.6 %all-reduce.40.cloned.1.call-start = ((), (), s32[]{:S(2)}) async-start(), calls=%async_computation.1 | async-start | bytes 25165824 | tf_op jit(solution)/shard_map/psum | solution.py:77
  353.7 3.6 collective-permute-start.2
  354.5 4.4 collective-permute-start.3
Sparse Core Ops, SparseCore 0:
  100.9 27.1 all-gather.1
  281.5 71.1 all-reduce.41
  387.1 181.8 all-reduce.39
where the time goes:
time: 600 us; the launch traced here: 588 us
  waiting for transfers between devices  301 us (50%)
  local copies, waits for them, and re-layouts  177 us (30%)
  other arithmetic  85.7 us (14%)
  between operations  19.5 us (3%)
    psum x1, waiting for transfers between devices, per_device(): summed = lax.psum(unsheared, 'angle')  182 us
    dynamic_update_slice x1, local copies, waits for them, and re-layouts, frame_loss(): window = jnp.roll(projected, (-offset[0], -offset[1]), axis=(1, 2))  96.8 us
    unnamed x4, waiting for transfers between devices  70.1 us
    gather x2, local copies, waits for them, and re-layouts, unshear_rows(): return lax.dynamic_slice_in_dim(rim_block, SH - amount, strip_rows, 1)  27.8 us
    concatenate x2, other arithmetic, with_halo(): x = jnp.concatenate([before, x, after], axis=dim)  26.2 us
    ppermute x2, waiting for transfers between devices, with_halo(): before = lax.ppermute(last, axis, up)  23 us
    all_gather x1, waiting for transfers between devices, per_device(): projected = lax.all_gather(own_strip, 'block', axis=1, tiled=True)  21.5 us
    unnamed x17, local copies, waits for them, and re-layouts  17.8 us
  transfers between devices with their start and end apart: 7, of which 6 were waited for; matrix products, arithmetic and copies ran while one was open for 0% of the time, Pallas kernels for 0%

commit v1 on v0

--- a/solution.py
+++ b/solution.py
@@ -7,6 +7,28 @@
 NY = 512
 STEPS = 2
 SH = 16
+
+
+def laid_out(parts, dim):
+    dims = list(parts.shape[1:])
+    dims[dim] *= parts.shape[0]
+    return jnp.moveaxis(parts, 0, dim).reshape(dims)
+
+
+def ring_gather(value, axis, dim):
+    devices = lax.axis_size(axis)
+    pairs = [(i, (i + 1) % devices) for i in range(devices)]
+    back = [(b, a) for a, b in pairs]
+    lower, upper = ([], [])
+    for step in range(devices - 1):
+        if step % 2 == 0:
+            lower.append(lax.ppermute(lower[-1] if lower else value, axis, pairs))
+        else:
+            upper.append(lax.ppermute(upper[-1] if upper else value, axis, back))
+    blocks = jnp.stack([*lower[::-1], value, *upper])
+    shift = lax.axis_index(axis) - len(lower)
+    blocks = blocks[(jnp.arange(devices) - shift) % devices]
+    return laid_out(blocks, dim)
 
 
 def with_halo(x, sides, width):
@@ -54,7 +76,7 @@
         return lax.dynamic_slice_in_dim(slab, SH + amount, strip_rows, 1)
 
     own_strip = jnp.sum(jax.vmap(slice_rows)(extended, shear_row), axis=0)
-    projected = lax.all_gather(own_strip, "block", axis=1, tiled=True)
+    projected = ring_gather(own_strip, "block", 1)
     intensity = probe_field[0] * probe_field[0] + probe_field[1] * probe_field[1]
     kappa_row = kappa_field[0]
 

time: 600 us -> 587 us (0.978)
  other arithmetic: 85.7 us -> 65.4 us
  starting transfers between devices: 5.85 us -> 20.3 us
  waiting for transfers between devices: 301 us -> 287 us
  local copies, waits for them, and re-layouts: 177 us -> 185 us
    all_gather x1 -> x0, waiting for transfers between devices: 21.5 us -> none  [per_device(): projected = lax.all_gather(own_strip, 'block', axis=1, tiled=True)]
    ppermute x0 -> x7, starting transfers between devices: none -> 14.8 us  [the longest x3 7.7 us: ring_gather(): upper.append(lax.ppermute(upper[-1] if upper else value, axis, back))]
    sub x1, other arithmetic: 12.8 us -> 1.37 us  [frame_loss(): real_part - kappa_row * laplace(imag_part)]
    concatenate x2, other arithmetic: 10.2 us -> 1.85 us  [frame_loss(): window = jnp.roll(projected, (-offset[0], -offset[1]), axis=(1, 2))]
    unnamed x17 -> x24, local copies, waits for them, and re-layouts: 17.8 us -> 24.6 us
    ppermute x0 -> x7, waiting for transfers between devices: none -> 6.5 us  [the longest x4 6.2 us: ring_gather(): lower.append(lax.ppermute(lower[-1] if lower else value, axis, pairs))]
    unnamed x4 -> x3, waiting for transfers between devices: 70.1 us -> 71.9 us
  transfers between devices with their start and end apart: 7 -> 13, of which waited for: 6 -> 10; matrix products, arithmetic and copies ran while one was open for 0% -> 1% of each run, Pallas kernels for 0% -> 0%
where the time goes in v1:
time: 587 us; the launch traced here: 577 us
  waiting for transfers between devices  287 us (49%)
  local copies, waits for them, and re-layouts  185 us (32%)
  other arithmetic  65.4 us (11%)
  starting transfers between devices  20.3 us (3%)
  between operations  19.6 us (3%)
    psum x1, waiting for transfers between devices, per_device(): summed = lax.psum(unsheared, 'angle')  182 us
    dynamic_update_slice x1, local copies, waits for them, and re-layouts, frame_loss(): window = jnp.roll(projected, (-offset[0], -offset[1]), axis=(1, 2))  97 us
    unnamed x3, waiting for transfers between devices  71.9 us
    gather x2, local copies, waits for them, and re-layouts, unshear_rows(): return lax.dynamic_slice_in_dim(rim_block, SH - amount, strip_rows, 1)  27.8 us
    concatenate x2, other arithmetic, with_halo(): x = jnp.concatenate([before, x, after], axis=dim)  26.1 us
    unnamed x24, local copies, waits for them, and re-layouts  24.6 us
    ppermute x2, waiting for transfers between devices, with_halo(): before = lax.ppermute(last, axis, up)  23.6 us
    gather x1, local copies, waits for them, and re-layouts, slice_rows(): return lax.dynamic_slice_in_dim(slab, SH + amount, strip_rows, 1)  16.4 us
  transfers between devices with their start and end apart: 13, of which 10 were waited for; matrix products, arithmetic and copies ran while one was open for 1% of the time, Pallas kernels for 0%

profile of v1, /device:TPU:1, one launch (start us, length us, event | category | flops | bytes accessed | tf_op | source)
XLA Modules:
  0.0 577.3 jit_solution(3759624508228548784)
XLA Ops:
  6.5 14.3 %copy.36 = f32[32,2,64,512]{3,1,0,2:T(2,128)S(1)} copy(f32[32,2,64,512]{3,2,1,0:T(8,128)} %param.6) | data formatting | bytes 16777216 | tf_op args[0]
  20.9 2.3 fusion.43
  23.2 3.0 collective-permute-start
  26.2 23.0 %collective-permute-done = f32[32,2,16,512]{3,1,0,2:T(2,128)S(1)} collective-permute-done((f32[32,2,16,512]{3,1,0,2:T(2,128)S(1)}, f32[32,2,16,512]{3,1,0,2:T(2,128)S(1)}, u32[]{:S(2)}, u32[]{:S(2)}) %collective-permute-start) | collective-permute-done | bytes 2097184 | tf_op jit(solution)/shard_map/ppermute | solution.py:41
  49.2 2.5 collective-permute-done.1
  51.7 26.0 %pad_maximum_fusion = f32[32,2,96,512]{3,1,0,2:T(2,128)} fusion(f32[32,2,16,512]{3,1,0,2:T(2,128)S(1)} %collective-permute-done.1, f32[32,2,64,512]{3,1,0,2:T(2,128)S(1)} %copy.36, f32[32,2,16,512]{3,1,0,2:T(2,128)S(1)} %collective-permute-done), kind=kLoop, calls=%fused_computation.3 | loop fusion | flops 6291456 | bytes 25165824 | tf_op jit(solution)/shard_map/concatenate | solution.py:43
  77.6 16.4 %gather_fusion.2 = f32[32,2,64,512]{3,1,2,0:T(2,128)} fusion(f32[32,2,96,512]{3,1,0,2:T(2,128)} %pad_maximum_fusion, s32[32]{0:T(128)S(1)} %get-tuple-element.113), kind=kCustom, calls=%fused_computation.2 | custom fusion | bytes 16777728 | tf_op jit(solution)/shard_map/vmap()/gather | solution.py:76
  94.1 6.1 %reduce_sum.9 = f32[2,64,512]{2,0,1:T(2,128)S(1)} reduce(f32[32,2,64,512]{3,1,2,0:T(2,128)} %gather_fusion.2, f32[]{:T(128)} %constant.118.clone.1), dimensions={0}, to_apply=%region_0.0 | reduce | flops 2031616 | bytes 8650756 | tf_op jit(solution)/shard_map/reduce_sum | solution.py:78
  100.2 3.3 collective-permute-done.2
  103.6 2.5 collective-permute-start.3
  106.0 1.4 collective-permute-start.6
  107.5 1.9 collective-permute-done.3
  109.4 2.5 collective-permute-start.4
  112.1 2.4 collective-permute-start.7
  114.5 1.0 collective-permute-done.4
  115.5 2.1 collective-permute-start.5
  123.1 3.9 collective-permute-start.8
  127.0 0.7 bitcast_dynamic-update-slice_fusion.7
  129.9 0.8 bitcast_dynamic-update-slice_fusion.3
  132.1 0.7 bitcast_dynamic-update-slice_fusion
  132.8 2.3 gather_fusion
  136.0 1.2 fusion.2
  138.9 0.8 copy-done
  139.7 1.4 fusion.16
  142.4 1.0 fusion.11
  144.6 2.5 bitcast_multiply_fusion.3
  148.4 1.2 bitcast_multiply_fusion.1
  151.1 2.4 fusion.34
  154.5 1.0 fusion.35
  156.4 1.6 copy.43
  158.0 3.1 broadcast_in_dim.38
  161.1 97.0 %dynamic_update_slice.10 = f32[2,512,1024]{2,0,1:T(2,128)} dynamic-update-slice(f32[2,512,1024]{2,0,1:T(2,128)} %broadcast_in_dim.38, f32[2,512,512]{2,0,1:T(2,128)S(1)} %copy.43, s32[]{:T(128)} %constant.119.clone.1, s32[]{:T(128)} %constant.119.clone.1, s32[]{:T(128)S(6)} %select_n.104) | dynamic-update-slice | bytes 4194308 | tf_op jit(solution)/shard_map/while/body/eval_jaxpr/transpose(jvp(jit(_roll_dynamic)))/dynamic_update_slice | solution.py:58
  258.2 1.1 broadcast_in_dim.37
  259.3 1.1 copy-done.2
  260.4 1.2 fusion.4
  261.6 1.1 slice_add_fusion.1
  263.8 0.7 broadcast_in_dim.43
  264.5 3.9 pad_maximum_fusion.1
  270.4 71.9 %all-reduce.42.cloned.1.call-done = f32[3,512,512]{2,0,1:T(4,128)} async-done(((f32[3,512,512]{2,0,1:T(4,128)}), f32[3,512,512]{2,0,1:T(4,128)}) %all-reduce.42.cloned.1.call-update) | async-done | bytes 3145744
  342.2 1.0 constant_dynamic-slice_fusion.1
  343.3 2.4 collective-permute-start.10
  345.7 1.1 constant_dynamic-slice_fusion.2
  346.8 0.8 collective-permute-done.10
  348.5 12.3 %gather_fusion.1 = f32[32,3,64,512]{3,1,2,0:T(4,128)} fusion(f32[3,96,512]{2,0,1:T(4,128)S(1)} %pad_maximum_fusion.2, s32[32]{0:T(128)S(1)} %get-tuple-element.112), kind=kCustom, calls=%fused_computation.1 | custom fusion | bytes 25166208 | tf_op jit(solution)/shard_map/vmap()/gather | solution.py:96
  360.7 15.5 %copy.44 = f32[32,3,64,512]{3,2,1,0:T(8,128)} copy(f32[32,3,64,512]{3,1,2,0:T(4,128)} %gather_fusion.1) | data formatting | bytes 25165824 | tf_op jit(solution)/shard_map/vmap()/gather | solution.py:96
  376.2 181.6 %all-reduce.40.cloned.1.call-done = f32[32,3,64,512]{3,2,1,0:T(8,128)} async-done(((f32[32,3,64,512]{3,2,1,0:T(8,128)}), f32[32,3,64,512]{3,2,1,0:T(8,128)}) %all-reduce.40.cloned.1.call-update) | async-done | bytes 12582928 | tf_op jit(solution)/shard_map/psum | solution.py:99
  557.9 2.9 fusion.1
  560.7 9.6 %fusion = f32[32,2,64,512]{3,2,1,0:T(8,128)} fusion(f32[32,2,64,512]{3,2,1,0:T(8,128)} %param.6, f32[32,3,64,512]{3,2,1,0:T(8,128)} %all-reduce.40.cloned.1.call-done, f32[32,64,512]{2,1,0:T(8,128)S(1)} %fusion.1), kind=kLoop, calls=%fused_computation.5 | loop fusion | flops 4194304 | bytes 29360128 | tf_op jit(solution)/shard_map/sub | solution.py:100
  (73 shorter events, 17.4 us)
Async XLA Ops:
  6.5 335.7 %all-reduce.42.cloned.1.call-start = ((), (), s32[]{:S(2)}) async-start(), calls=%async_computation.1 | async-start | bytes 8388608
  20.9 5.4 copy-start.5
  23.2 26.0 %collective-permute-start = (f32[32,2,16,512]{3,1,0,2:T(2,128)S(1)}, f32[32,2,16,512]{3,1,0,2:T(2,128)S(1)}, u32[]{:S(2)}, u32[]{:S(2)}) collective-permute-start(f32[32,2,16,512]{3,1,0,2:T(2,128)S(1)} %get-tuple-element.41), channel_id=1, source_target_pairs={{0,1},{1,2},{2,3},{3,4},{4,5},{5,6},{6,7},{7,0},{8,9},{9,10},{10,1... | collective-permute-start | bytes 6291464 | tf_op jit(solution)/shard_map/ppermute | solution.py:41
  26.2 25.5 %collective-permute-start.1 = (f32[32,2,16,512]{3,1,0,2:T(2,128)S(1)}, f32[32,2,16,512]{3,1,0,2:T(2,128)S(1)}, u32[]{:S(2)}, u32[]{:S(2)}) collective-permute-start(f32[32,2,16,512]{3,1,0,2:T(2,128)S(1)} %get-tuple-element.42), channel_id=1, source_target_pairs={{1,0},{2,1},{3,2},{4,3},{5,4},{6,5},{7,6},{0,7},{9,8},{10,9},{11,1... | collective-permute-start | bytes 6291464 | tf_op jit(solution)/shard_map/ppermute | solution.py:42
  94.0 23.6 %copy-start.4 = (s32[1,1,2]{2,1,0:T(1,128)S(1)}, s32[1,1,2]{2,1,0:T(1,128)}, u32[]{:S(2)}) copy-start(s32[1,1,2]{2,1,0:T(1,128)} %param.8) | copy-start | bytes 28
  100.2 3.3 collective-permute-start.2
  103.6 5.8 %collective-permute-start.3 = (f32[2,64,512]{2,1,0:T(8,128)S(1)}, f32[2,64,512]{2,1,0:T(8,128)S(1)}, u32[]{:S(2)}, u32[]{:S(2)}) collective-permute-start(f32[2,64,512]{2,1,0:T(8,128)S(1)} %collective-permute-done.2), channel_id=1, source_target_pairs={{0,1},{1,2},{2,3},{3,4},{4,5},{5,6},{6,7},{7,0},{8,9},{9,10},{10,1... | collective-permute-start | bytes 786440 | tf_op jit(solution)/shard_map/ppermute | solution.py:25
  106.0 6.1 %collective-permute-start.6 = (f32[2,64,512]{2,1,0:T(8,128)S(1)}, f32[2,64,512]{2,1,0:T(8,128)S(1)}, u32[]{:S(2)}, u32[]{:S(2)}) collective-permute-start(f32[2,64,512]{2,1,0:T(8,128)S(1)} %copy.39), channel_id=1, source_target_pairs={{1,0},{2,1},{3,2},{4,3},{5,4},{6,5},{7,6},{0,7},{9,8},{10,9},{11,1... | collective-permute-start | bytes 786440 | tf_op jit(solution)/shard_map/ppermute | solution.py:27
  109.4 6.2 %collective-permute-start.4 = (f32[2,64,512]{2,1,0:T(8,128)S(1)}, f32[2,64,512]{2,1,0:T(8,128)S(1)}, u32[]{:S(2)}, u32[]{:S(2)}) collective-permute-start(f32[2,64,512]{2,1,0:T(8,128)S(1)} %collective-permute-done.3), channel_id=1, source_target_pairs={{0,1},{1,2},{2,3},{3,4},{4,5},{5,6},{6,7},{7,0},{8,9},{9,10},{10,1... | collective-permute-start | bytes 786440 | tf_op jit(solution)/shard_map/ppermute | solution.py:25
  112.1 11.0 %collective-permute-start.7 = (f32[2,64,512]{2,1,0:T(8,128)S(1)}, f32[2,64,512]{2,1,0:T(8,128)S(1)}, u32[]{:S(2)}, u32[]{:S(2)}) collective-permute-start(f32[2,64,512]{2,1,0:T(8,128)S(1)} %collective-permute-done.6), channel_id=1, source_target_pairs={{1,0},{2,1},{3,2},{4,3},{5,4},{6,5},{7,6},{0,7},{9,8},{10,9},{11,1... | collective-permute-start | bytes 786440 | tf_op jit(solution)/shard_map/ppermute | solution.py:27
  115.5 11.5 %collective-permute-start.5 = (f32[2,64,512]{2,1,0:T(8,128)S(1)}, f32[2,64,512]{2,1,0:T(8,128)S(1)}, u32[]{:S(2)}, u32[]{:S(2)}) collective-permute-start(f32[2,64,512]{2,1,0:T(8,128)S(1)} %collective-permute-done.4), channel_id=1, source_target_pairs={{0,1},{1,2},{2,3},{3,4},{4,5},{5,6},{6,7},{7,0},{8,9},{9,10},{10,1... | collective-permute-start | bytes 786440 | tf_op jit(solution)/shard_map/ppermute | solution.py:25
  123.1 9.0 %collective-permute-start.8 = (f32[2,64,512]{2,1,0:T(8,128)S(1)}, f32[2,64,512]{2,1,0:T(8,128)S(1)}, u32[]{:S(2)}, u32[]{:S(2)}) collective-permute-start(f32[2,64,512]{2,1,0:T(8,128)S(1)} %collective-permute-done.7), channel_id=1, source_target_pairs={{1,0},{2,1},{3,2},{4,3},{5,4},{6,5},{7,6},{0,7},{9,8},{10,9},{11,1... | collective-permute-start | bytes 786440 | tf_op jit(solution)/shard_map/ppermute | solution.py:27
  136.0 1.6 copy-start.1
  138.4 1.2 copy-start
  143.6 1.0 copy-start.3
  258.2 2.2 copy-start.2
  268.4 0.7 copy-start.6
  268.5 289.4 %all-reduce.40.cloned.1.call-start = ((), (), s32[]{:S(2)}) async-start(), calls=%async_computation | async-start | bytes 25165824 | tf_op jit(solution)/shard_map/psum | solution.py:99
  343.3 4.4 collective-permute-start.10
  345.7 2.6 collective-permute-start.9
Sparse Core Ops, SparseCore 0:
  268.6 73.6 all-reduce.41
  376.4 181.4 all-reduce.39
